TPU v7x, 32 devices: a whole 2x2x4 slice. The times are simulated.
32 devices in a mesh: section: 4 (over y, x), coil: 2 (over core), space: 4 (over z).
Axes of the slice: x: 2, y: 2, z: 4, core: 2. Of those that a mesh axis runs over, the one named last changes fastest.
Arguments:
- image: float32 [4, 2, 2, 256, 256], P(None, None, 'coil', 'space'), may hold values from -6 to 6
- sens: bfloat16 [4, 2, 2, 256, 512], P('coil', None, None, 'space'), may hold values from -2 to 2
- adjoint: float32 [4, 2, 2, 256, 256], P(None, None, 'coil', 'space'), may hold values from -6 to 6
- mask_bits: int32 [2, 256, 9], replicated, may hold values from 0 to 1073741823, as said below
- step_size: float32 [4], P('section'), may hold values from 0.3 to 1
- conv1_w: bfloat16 [4, 32, 108], P('section'), may hold values from -0.625 to 0.625
- conv1_b: float32 [4, 32], P('section'), may hold values from -1 to 1
- conv2_w: bfloat16 [4, 32, 108], P('section'), may hold values from -0.125 to 0.125
Outputs:
- cascade_images: float32 [4, 4, 2, 2, 256, 256], P('section', None, None, 'coil', 'space')
Inputs may be any that keep to these rules, and one draw needn't show every extreme that they name: `mask_bits`: bit b of word w in row (p, ky) is 1 where k-space point (ky, 30 w + b) is sampled in phase p; bits for points at or beyond 256 are 0.
All inputs are finite; a program needn't handle non-finite values.
Results may differ from a plain program's by a relative error of at most 0.01.
Values may be sent and summed in bfloat16 or wider, within the bound.
No kernel may reach another device: no remote copies, remote signals or barrier semaphores. Data moves between devices by JAX's collectives and lax.ppermute only.
A program may use at most 128 MiB of HBM per device.

v0:
```python
import math
import jax
import jax.numpy as jnp
from jax import lax
from jax.sharding import PartitionSpec as P


def extended(cells, sides, width):
    for axis, dim in sides:
        count = lax.axis_size(axis)
        ends = count - 1
        head = lax.slice_in_dim(cells, 0, width, axis=dim)
        tail = lax.slice_in_dim(cells, cells.shape[dim] - width, cells.shape[dim], axis=dim)
        cells = jnp.concatenate(
            [
                lax.ppermute(tail, axis, [(i, (i + 1) % count) for i in range(ends)]),
                cells,
                lax.ppermute(head, axis, [((i + 1) % count, i) for i in range(ends)]),
            ],
            axis=dim,
        )
    return cells


def passed_along(value, axis, steps):
    count = lax.axis_size(axis)
    leading, last = (max(0, -steps), min(count, count - steps))
    return lax.ppermute(value, axis, [(source, source + steps) for source in range(leading, last)])


def dft_tables(length):
    index = jnp.arange(length, dtype=jnp.int32)
    product = index[:, None] * index[None, :] % length
    angle = product.astype(jnp.float32) * (2.0 * math.pi / length)
    scale = 1.0 / math.sqrt(length)
    return (
        (jnp.cos(angle) * scale).astype(jnp.bfloat16),
        (jnp.sin(angle) * scale).astype(jnp.bfloat16),
    )


def unpack_mask(mask_bits, length_z):
    column = jnp.arange(length_z, dtype=jnp.int32)
    word_count = mask_bits.shape[2]
    select = (column[:, None] // 30 == jnp.arange(word_count, dtype=jnp.int32)[None, :]).astype(
        jnp.int32
    )
    chosen = jnp.sum(mask_bits[:, :, None, :] * select[None, None], axis=3)
    return (jnp.right_shift(chosen, column % 30) & 1).astype(jnp.float32)


def mult_last(values, table):
    return jnp.einsum("...n,nk->...k", values, table, preferred_element_type=jnp.float32)


def mult_rows(values, table):
    return jnp.einsum("kn,...nz->...kz", table, values, preferred_element_type=jnp.float32)


def along_last(real_part, imag_part, cos_table, sin_table, direction):
    first = mult_last(real_part, cos_table) + direction * mult_last(imag_part, sin_table)
    second = mult_last(imag_part, cos_table) - direction * mult_last(real_part, sin_table)
    return (first, second)


def along_rows(real_part, imag_part, cos_table, sin_table, direction):
    first = mult_rows(real_part, cos_table) + direction * mult_rows(imag_part, sin_table)
    second = mult_rows(imag_part, cos_table) - direction * mult_rows(real_part, sin_table)
    return (first, second)


def correlate(source, weights):
    channels = source.shape[0]
    out_x = source.shape[1] - 2
    out_y = source.shape[2] - 2
    length_z = source.shape[3]
    padded = jnp.pad(source, ((0, 0), (0, 0), (0, 0), (1, 1)))
    result = jnp.zeros((weights.shape[0], out_x, out_y, length_z), jnp.float32)
    for offset_x in range(3):
        pieces = []
        for offset_y in range(3):
            for offset_z in range(3):
                pieces.append(
                    padded[
                        :,
                        offset_x : offset_x + out_x,
                        offset_y : offset_y + out_y,
                        offset_z : offset_z + length_z,
                    ]
                )
        patches = jnp.stack(pieces, axis=0).reshape(9 * channels, out_x, out_y, length_z)
        weight_block = weights[:, offset_x * 9 * channels : (offset_x + 1) * 9 * channels]
        result = result + jnp.einsum(
            "ok,kxyz->oxyz", weight_block, patches, preferred_element_type=jnp.float32
        )
    return result


def per_device(image, sens, adjoint, mask_bits, step_size, conv1_w, conv1_b, conv2_w):
    channels = image.shape[0]
    slab_count = image.shape[1]
    row_count = image.shape[3]
    length_z = image.shape[4]
    phases = mask_bits.shape[0]
    length_y = mask_bits.shape[1]
    planes = lax.axis_size("coil")
    spaces = lax.axis_size("space")
    coil_local = sens.shape[0]
    item_count = coil_local * planes * phases
    item_local = item_count // spaces
    hidden_width = conv1_w.shape[1]
    section_index = lax.axis_index("section")
    space_index = lax.axis_index("space")
    sampled = unpack_mask(mask_bits, length_z)
    cos_z, sin_z = dft_tables(length_z)
    cos_y, sin_y = dft_tables(length_y)
    step_rate = step_size[0]
    first_w = conv1_w[0]
    bias_one = conv1_b[0]
    second_w = (
        conv2_w[0]
        .reshape(hidden_width, 27, channels)
        .transpose(2, 1, 0)
        .reshape(channels, 27 * hidden_width)
    )
    item_ids = space_index * item_local + jnp.arange(item_local, dtype=jnp.int32)
    phase_pick = (
        item_ids[:, None] % phases == jnp.arange(phases, dtype=jnp.int32)[None, :]
    ).astype(jnp.float32)
    item_mask = jnp.einsum("kp,pyz->kyz", phase_pick, sampled)

    def cascade(current, slab_index):
        coil_maps = lax.dynamic_index_in_dim(sens, slab_index, 1, keepdims=False)
        coil_maps = coil_maps.reshape(coil_local, planes, row_count, 2, length_z)
        map_re = coil_maps[:, :, :, 0].astype(jnp.float32)[:, :, None]
        map_im = coil_maps[:, :, :, 1].astype(jnp.float32)[:, :, None]
        adjoint_slab = lax.dynamic_index_in_dim(adjoint, slab_index, 1, keepdims=False)
        gathered = lax.all_gather(current.astype(jnp.bfloat16), "coil", axis=1, tiled=True)
        planar = (
            gathered.reshape(phases, 2, planes, row_count, length_z)
            .transpose(2, 0, 1, 3, 4)
            .astype(jnp.float32)
        )
        image_re = planar[:, :, 0][None]
        image_im = planar[:, :, 1][None]
        coil_re = (map_re * image_re - map_im * image_im).astype(jnp.bfloat16)
        coil_im = (map_re * image_im + map_im * image_re).astype(jnp.bfloat16)
        coil_img = jnp.stack([coil_re, coil_im], axis=3).reshape(item_count, 2, row_count, length_z)
        exchanged = lax.all_to_all(coil_img, "space", split_axis=0, concat_axis=2, tiled=True)
        fwd_re, fwd_im = along_last(exchanged[:, 0], exchanged[:, 1], cos_z, sin_z, 1.0)
        spec_re, spec_im = along_rows(
            fwd_re.astype(jnp.bfloat16), fwd_im.astype(jnp.bfloat16), cos_y, sin_y, 1.0
        )
        spec_re = (spec_re * item_mask).astype(jnp.bfloat16)
        spec_im = (spec_im * item_mask).astype(jnp.bfloat16)
        inv_re, inv_im = along_rows(spec_re, spec_im, cos_y, sin_y, -1.0)
        out_re, out_im = along_last(
            inv_re.astype(jnp.bfloat16), inv_im.astype(jnp.bfloat16), cos_z, sin_z, -1.0
        )
        outgoing = jnp.stack([out_re.astype(jnp.bfloat16), out_im.astype(jnp.bfloat16)], axis=1)
        returned_img = lax.all_to_all(outgoing, "space", split_axis=2, concat_axis=0, tiled=True)
        returned_img = returned_img.reshape(
            coil_local, planes, phases, 2, row_count, length_z
        ).astype(jnp.float32)
        back_re = returned_img[:, :, :, 0]
        back_im = returned_img[:, :, :, 1]
        part_re = jnp.sum(map_re * back_re + map_im * back_im, axis=0)
        part_im = jnp.sum(map_re * back_im - map_im * back_re, axis=0)
        partial_value = (
            jnp.stack([part_re, part_im], axis=2)
            .transpose(1, 2, 0, 3, 4)
            .reshape(channels, planes, row_count, length_z)
        )
        shares = lax.psum_scatter(
            partial_value.astype(jnp.bfloat16), "coil", scatter_dimension=1, tiled=True
        ).astype(jnp.float32)
        updated = current - step_rate * (shares - adjoint_slab)
        lifted = updated.astype(jnp.bfloat16)
        widened = extended(lifted, (("coil", 1), ("space", 2)), 1)
        hidden = jnp.maximum(
            correlate(widened, first_w) + bias_one[:, None, None, None], 0.0
        ).astype(jnp.bfloat16)
        hidden_wide = extended(hidden, (("coil", 1), ("space", 2)), 1)
        return updated + correlate(hidden_wide, second_w)

    tick_count = slab_count + lax.axis_size("section") - 1

    def advance(tick_index, loop_state):
        incoming, outputs = loop_state
        offset = tick_index - section_index
        slab_index = jnp.clip(offset, 0, slab_count - 1)
        entering = lax.dynamic_index_in_dim(image, slab_index, 1, keepdims=False)
        current = jnp.where(section_index == 0, entering, incoming)
        finished = cascade(current, slab_index)
        active = (offset >= 0) & (offset < slab_count)
        previous = lax.dynamic_index_in_dim(outputs, slab_index, 1, keepdims=True)
        stored = jnp.where(active, finished[:, None], previous)
        outputs = lax.dynamic_update_slice_in_dim(outputs, stored, slab_index, 1)
        passed = passed_along(finished.astype(jnp.bfloat16), "section", 1).astype(finished.dtype)
        return (passed, outputs)

    initial = (jnp.zeros_like(image[:, 0]), jnp.zeros_like(image))
    last_in, outputs = lax.fori_loop(0, tick_count, advance, initial)
    return outputs[None]


def solution(mesh):
    in_specs = (
        P(None, None, "coil", "space", None),
        P("coil", None, None, "space", None),
        P(None, None, "coil", "space", None),
        P(),
        P("section"),
        P("section", None, None),
        P("section", None),
        P("section", None, None),
    )
    out_specs = P("section", None, None, "coil", "space", None)
    return jax.shard_map(
        per_device, mesh=mesh, in_specs=in_specs, out_specs=out_specs, check_vma=False
    )
```

profile of v0, /device:TPU:20, one launch (start us, length us, event | category | flops | bytes accessed | tf_op | source)
XLA Modules:
  0.0 1037.9 jit_solution(15423953089467877045)
XLA Ops:
  10.2 1020.9 %while.20 = (s32[]{:T(128)}, f32[4,1,64,256]{3,0,2,1:T(4,128)S(1)}, f32[4,2,1,64,256]{4,3,1,0,2:T(8,128)}, pred[]{:T(512)}, s32[]{:T(128)}, /*index=5*/f32[4,2,1...) while((s32[]{:T(128)}, f32[4,1,64,256]{3,0,2,1:T(4,128)S(1)}, ...), condition=%wide.region_5.6_spmd.clone.clone, body=%wide.region_1.5_spmd.clone.clone.sunk | while | flops 1387907712 | bytes 364505152 | solution.py:203
  15.4 17.1 %all_to_all.86 = bf16[8,2,64,256]{3,2,1,0:T(8,128)(2,1)S(1)} all-to-all(bf16[8,2,64,256]{3,2,1,0:T(8,128)(2,1)S(1)} %copy.304), channel_id=1, replica_groups=mesh['section'=4,'coil'=2,'space'=4] {'space'}, dimensions={0} | all-to-all | bytes 1048576 | tf_op jit(solution)/shard_map/while/body/eval_jaxpr/all_to_all | solution.py:149
  52.8 16.6 %all_to_all.87 = bf16[2,2,256,256]{3,0,1,2:T(2,128)(2,1)S(1)} all-to-all(bf16[2,2,256,256]{3,0,1,2:T(2,128)(2,1)S(1)} %copy.306), channel_id=1, replica_groups=mesh['section'=4,'coil'=2,'space'=4] {'space'}, dimensions={2} | all-to-all | bytes 1048576 | tf_op jit(solution)/shard_map/while/body/eval_jaxpr/all_to_all | solution.py:161
  143.8 13.3 %copy.313 = bf16[9,32,1,64,256]{4,3,1,0,2:T(8,128)(2,1)} copy(bf16[9,32,1,64,256]{4,1,3,2,0:T(8,128)(2,1)} %fusion.424) | data formatting | bytes 18874368 | tf_op jit(solution)/shard_map/while/body/eval_jaxpr/stack | solution.py:91
  157.1 13.5 %copy.314 = bf16[9,32,1,64,256]{4,3,1,0,2:T(8,128)(2,1)} copy(bf16[9,32,1,64,256]{4,1,3,2,0:T(8,128)(2,1)} %copy-done.1) | data formatting | bytes 18874368 | tf_op jit(solution)/shard_map/while/body/eval_jaxpr/stack | solution.py:91
  184.9 13.3 %copy.315 = bf16[9,32,1,64,256]{4,3,1,0,2:T(8,128)(2,1)} copy(bf16[9,32,1,64,256]{4,1,3,2,0:T(8,128)(2,1)} %copy-done) | data formatting | bytes 18874368 | tf_op jit(solution)/shard_map/while/body/eval_jaxpr/stack | solution.py:91
  220.3 17.0 %all_to_all.86 = bf16[8,2,64,256]{3,2,1,0:T(8,128)(2,1)S(1)} all-to-all(bf16[8,2,64,256]{3,2,1,0:T(8,128)(2,1)S(1)} %copy.304), channel_id=1, replica_groups=mesh['section'=4,'coil'=2,'space'=4] {'space'}, dimensions={0} | all-to-all | bytes 1048576 | tf_op jit(solution)/shard_map/while/body/eval_jaxpr/all_to_all | solution.py:149
  257.4 16.6 %all_to_all.87 = bf16[2,2,256,256]{3,0,1,2:T(2,128)(2,1)S(1)} all-to-all(bf16[2,2,256,256]{3,0,1,2:T(2,128)(2,1)S(1)} %copy.306), channel_id=1, replica_groups=mesh['section'=4,'coil'=2,'space'=4] {'space'}, dimensions={2} | all-to-all | bytes 1048576 | tf_op jit(solution)/shard_map/while/body/eval_jaxpr/all_to_all | solution.py:161
  347.6 13.3 %copy.313 = bf16[9,32,1,64,256]{4,3,1,0,2:T(8,128)(2,1)} copy(bf16[9,32,1,64,256]{4,1,3,2,0:T(8,128)(2,1)} %fusion.424) | data formatting | bytes 18874368 | tf_op jit(solution)/shard_map/while/body/eval_jaxpr/stack | solution.py:91
  360.9 13.5 %copy.314 = bf16[9,32,1,64,256]{4,3,1,0,2:T(8,128)(2,1)} copy(bf16[9,32,1,64,256]{4,1,3,2,0:T(8,128)(2,1)} %copy-done.1) | data formatting | bytes 18874368 | tf_op jit(solution)/shard_map/while/body/eval_jaxpr/stack | solution.py:91
  388.7 13.3 %copy.315 = bf16[9,32,1,64,256]{4,3,1,0,2:T(8,128)(2,1)} copy(bf16[9,32,1,64,256]{4,1,3,2,0:T(8,128)(2,1)} %copy-done) | data formatting | bytes 18874368 | tf_op jit(solution)/shard_map/while/body/eval_jaxpr/stack | solution.py:91
  424.1 17.0 %all_to_all.86 = bf16[8,2,64,256]{3,2,1,0:T(8,128)(2,1)S(1)} all-to-all(bf16[8,2,64,256]{3,2,1,0:T(8,128)(2,1)S(1)} %copy.304), channel_id=1, replica_groups=mesh['section'=4,'coil'=2,'space'=4] {'space'}, dimensions={0} | all-to-all | bytes 1048576 | tf_op jit(solution)/shard_map/while/body/eval_jaxpr/all_to_all | solution.py:149
  461.3 16.6 %all_to_all.87 = bf16[2,2,256,256]{3,0,1,2:T(2,128)(2,1)S(1)} all-to-all(bf16[2,2,256,256]{3,0,1,2:T(2,128)(2,1)S(1)} %copy.306), channel_id=1, replica_groups=mesh['section'=4,'coil'=2,'space'=4] {'space'}, dimensions={2} | all-to-all | bytes 1048576 | tf_op jit(solution)/shard_map/while/body/eval_jaxpr/all_to_all | solution.py:161
  551.4 13.3 %copy.313 = bf16[9,32,1,64,256]{4,3,1,0,2:T(8,128)(2,1)} copy(bf16[9,32,1,64,256]{4,1,3,2,0:T(8,128)(2,1)} %fusion.424) | data formatting | bytes 18874368 | tf_op jit(solution)/shard_map/while/body/eval_jaxpr/stack | solution.py:91
  564.7 13.5 %copy.314 = bf16[9,32,1,64,256]{4,3,1,0,2:T(8,128)(2,1)} copy(bf16[9,32,1,64,256]{4,1,3,2,0:T(8,128)(2,1)} %copy-done.1) | data formatting | bytes 18874368 | tf_op jit(solution)/shard_map/while/body/eval_jaxpr/stack | solution.py:91
  592.4 13.3 %copy.315 = bf16[9,32,1,64,256]{4,3,1,0,2:T(8,128)(2,1)} copy(bf16[9,32,1,64,256]{4,1,3,2,0:T(8,128)(2,1)} %copy-done) | data formatting | bytes 18874368 | tf_op jit(solution)/shard_map/while/body/eval_jaxpr/stack | solution.py:91
  627.9 17.0 %all_to_all.86 = bf16[8,2,64,256]{3,2,1,0:T(8,128)(2,1)S(1)} all-to-all(bf16[8,2,64,256]{3,2,1,0:T(8,128)(2,1)S(1)} %copy.304), channel_id=1, replica_groups=mesh['section'=4,'coil'=2,'space'=4] {'space'}, dimensions={0} | all-to-all | bytes 1048576 | tf_op jit(solution)/shard_map/while/body/eval_jaxpr/all_to_all | solution.py:149
  665.0 16.6 %all_to_all.87 = bf16[2,2,256,256]{3,0,1,2:T(2,128)(2,1)S(1)} all-to-all(bf16[2,2,256,256]{3,0,1,2:T(2,128)(2,1)S(1)} %copy.306), channel_id=1, replica_groups=mesh['section'=4,'coil'=2,'space'=4] {'space'}, dimensions={2} | all-to-all | bytes 1048576 | tf_op jit(solution)/shard_map/while/body/eval_jaxpr/all_to_all | solution.py:161
  755.2 13.3 %copy.313 = bf16[9,32,1,64,256]{4,3,1,0,2:T(8,128)(2,1)} copy(bf16[9,32,1,64,256]{4,1,3,2,0:T(8,128)(2,1)} %fusion.424) | data formatting | bytes 18874368 | tf_op jit(solution)/shard_map/while/body/eval_jaxpr/stack | solution.py:91
  768.5 13.5 %copy.314 = bf16[9,32,1,64,256]{4,3,1,0,2:T(8,128)(2,1)} copy(bf16[9,32,1,64,256]{4,1,3,2,0:T(8,128)(2,1)} %copy-done.1) | data formatting | bytes 18874368 | tf_op jit(solution)/shard_map/while/body/eval_jaxpr/stack | solution.py:91
  831.7 17.0 %all_to_all.86 = bf16[8,2,64,256]{3,2,1,0:T(8,128)(2,1)S(1)} all-to-all(bf16[8,2,64,256]{3,2,1,0:T(8,128)(2,1)S(1)} %copy.304), channel_id=1, replica_groups=mesh['section'=4,'coil'=2,'space'=4] {'space'}, dimensions={0} | all-to-all | bytes 1048576 | tf_op jit(solution)/shard_map/while/body/eval_jaxpr/all_to_all | solution.py:149
  868.8 16.6 %all_to_all.87 = bf16[2,2,256,256]{3,0,1,2:T(2,128)(2,1)S(1)} all-to-all(bf16[2,2,256,256]{3,0,1,2:T(2,128)(2,1)S(1)} %copy.306), channel_id=1, replica_groups=mesh['section'=4,'coil'=2,'space'=4] {'space'}, dimensions={2} | all-to-all | bytes 1048576 | tf_op jit(solution)/shard_map/while/body/eval_jaxpr/all_to_all | solution.py:161
  959.0 13.3 %copy.313 = bf16[9,32,1,64,256]{4,3,1,0,2:T(8,128)(2,1)} copy(bf16[9,32,1,64,256]{4,1,3,2,0:T(8,128)(2,1)} %fusion.424) | data formatting | bytes 18874368 | tf_op jit(solution)/shard_map/while/body/eval_jaxpr/stack | solution.py:91
  972.3 13.5 %copy.314 = bf16[9,32,1,64,256]{4,3,1,0,2:T(8,128)(2,1)} copy(bf16[9,32,1,64,256]{4,1,3,2,0:T(8,128)(2,1)} %copy-done.1) | data formatting | bytes 18874368 | tf_op jit(solution)/shard_map/while/body/eval_jaxpr/stack | solution.py:91
  (623 shorter events, 678.1 us)
Async XLA Ops:
  10.2 69.6 %reduce-scatter.2.cloned.1.call-start = ((), (), s32[]{:S(2)}) async-start(), calls=%async_computation.3 | async-start | bytes 393216 | tf_op jit(solution)/shard_map/while/body/eval_jaxpr/reduce_scatter | solution.py:174
  87.8 5.9 collective-permute-start.2
  109.6 6.2 collective-permute-start.6
  112.0 6.2 collective-permute-start.7
  207.1 7.8 collective-permute-start.8
  215.1 68.5 %reduce-scatter.2.cloned.1.call-start = ((), (), s32[]{:S(2)}) async-start(), calls=%async_computation.3 | async-start | bytes 393216 | tf_op jit(solution)/shard_map/while/body/eval_jaxpr/reduce_scatter | solution.py:174
  291.6 5.9 collective-permute-start.2
  313.4 6.2 collective-permute-start.6
  315.8 6.2 collective-permute-start.7
  410.9 7.8 collective-permute-start.8
  418.9 68.5 %reduce-scatter.2.cloned.1.call-start = ((), (), s32[]{:S(2)}) async-start(), calls=%async_computation.3 | async-start | bytes 393216 | tf_op jit(solution)/shard_map/while/body/eval_jaxpr/reduce_scatter | solution.py:174
  495.4 5.9 collective-permute-start.2
  517.1 6.2 collective-permute-start.6
  519.6 6.2 collective-permute-start.7
  614.6 7.8 collective-permute-start.8
  622.7 68.5 %reduce-scatter.2.cloned.1.call-start = ((), (), s32[]{:S(2)}) async-start(), calls=%async_computation.3 | async-start | bytes 393216 | tf_op jit(solution)/shard_map/while/body/eval_jaxpr/reduce_scatter | solution.py:174
  699.2 5.9 collective-permute-start.2
  720.9 6.2 collective-permute-start.6
  723.4 6.2 collective-permute-start.7
  818.4 7.8 collective-permute-start.8
  826.5 68.5 %reduce-scatter.2.cloned.1.call-start = ((), (), s32[]{:S(2)}) async-start(), calls=%async_computation.3 | async-start | bytes 393216 | tf_op jit(solution)/shard_map/while/body/eval_jaxpr/reduce_scatter | solution.py:174
  924.7 6.2 collective-permute-start.6
  927.2 6.2 collective-permute-start.7
  1022.2 7.8 collective-permute-start.8
  (74 other events, 691.7 us)
Sparse Core Ops, SparseCore 0:
  70.6 9.1 reduce-scatter.1
  275.2 8.3 reduce-scatter.1
  479.0 8.2 reduce-scatter.1
  682.8 8.2 reduce-scatter.1
  886.6 8.3 reduce-scatter.1
where the time goes:
time: 1040 us
  local copies, waits for them, and re-layouts  328 us (32%)
  matrix products  227 us (22%)
  blocking collectives  178 us (17%)
  starting transfers between devices  120 us (12%)
  waiting for transfers between devices  98.9 us (10%)
  other arithmetic  67.8 us (7%)
  between operations  13.4 us (1%)
    another operation x45, local copies, waits for them, and re-layouts, correlate(): jnp.stack(pieces, axis=0).reshape(9 * channels, out_x, out_y, length_z)  223 us
    dot_general x30, matrix products, correlate(): jnp.einsum('ok,kxyz->oxyz', weight_block, patches, preferred_element_type...  130 us
    all_to_all x5, blocking collectives, cascade(): lax.all_to_all(coil_img, 'space', split_axis=0, concat_axis=2, tiled=True)  85 us
    all_to_all x5, blocking collectives, cascade(): lax.all_to_all(outgoing, 'space', split_axis=2, concat_axis=0, tiled=True)  83 us
    while x175, local copies, waits for them, and re-layouts  79.3 us
    ppermute x20, starting transfers between devices, extended(): lax.ppermute(tail, axis, [(i, (i + 1) % count) for i in range(ends)])  64.8 us
    dot_general x40, matrix products, mult_rows(): jnp.einsum('kn,...nz->...kz', table, values, preferred_element_type=jnp.f...  49.7 us
    dot_general x40, matrix products, mult_last(): jnp.einsum('...n,nk->...k', values, table, preferred_element_type=jnp.flo...  47.3 us
  transfers between devices with their start and end apart: 50, of which 40 were waited for; matrix products, arithmetic and copies ran while one was open for 1% of the time, Pallas kernels for 0%

commit v1 on v0

--- a/solution.py
+++ b/solution.py
@@ -3,6 +3,18 @@
 import jax.numpy as jnp
 from jax import lax
 from jax.sharding import PartitionSpec as P
+
+
+def split_up(x, dim, size):
+    lengths = x.shape
+    blocks = x.reshape(*lengths[:dim], size, lengths[dim] // size, *lengths[dim + 1 :])
+    return jnp.moveaxis(blocks, dim, 0)
+
+
+def joined_along(tiles, dim):
+    shape = list(tiles.shape[1:])
+    shape[dim] *= tiles.shape[0]
+    return jnp.moveaxis(tiles, 0, dim).reshape(shape)
 
 
 def extended(cells, sides, width):
@@ -158,7 +170,16 @@
             inv_re.astype(jnp.bfloat16), inv_im.astype(jnp.bfloat16), cos_z, sin_z, -1.0
         )
         outgoing = jnp.stack([out_re.astype(jnp.bfloat16), out_im.astype(jnp.bfloat16)], axis=1)
-        returned_img = lax.all_to_all(outgoing, "space", split_axis=2, concat_axis=0, tiled=True)
+        size, here = (lax.axis_size("space"), lax.axis_index("space"))
+        blocks = split_up(outgoing, 2, size)
+        finished_2 = [blocks[here]]
+        for step in range(1, size):
+            sent = blocks[here ^ step]
+            finished_2.append(
+                lax.ppermute(sent, "space", [(i_2, i_2 ^ step) for i_2 in range(size)])
+            )
+        blocks = jnp.stack(finished_2)[here ^ jnp.arange(size)]
+        returned_img = joined_along(blocks, 0)
         returned_img = returned_img.reshape(
             coil_local, planes, phases, 2, row_count, length_z
         ).astype(jnp.float32)

time: 1040 us -> 1030 us (level)
  blocking collectives: 178 us -> 9.97 us
  waiting for transfers between devices: 98.9 us -> 197 us
  starting transfers between devices: 120 us -> 170 us
    all_to_all x10 -> x0, blocking collectives: 168 us -> none  [the longest x5 85 us: cascade(): lax.all_to_all(coil_img, 'space', split_axis=0, concat_axis=2, tiled=True)]
    all_to_all x0 -> x5, waiting for transfers between devices: none -> 57.6 us  [cascade(): lax.all_to_all(coil_img, 'space', split_axis=0, concat_axis=2, tiled=True)]
    ppermute x0 -> x15, waiting for transfers between devices: none -> 39.6 us  [cascade(): lax.ppermute(sent, 'space', [(i_2, i_2 ^ step) for i_2 in range(size)])]
    all_to_all x0 -> x5, starting transfers between devices: none -> 25.7 us  [cascade(): lax.all_to_all(coil_img, 'space', split_axis=0, concat_axis=2, tiled=True)]
    ppermute x0 -> x15, starting transfers between devices: none -> 24.8 us  [cascade(): lax.ppermute(sent, 'space', [(i_2, i_2 ^ step) for i_2 in range(size)])]
  transfers between devices with their start and end apart: 50 -> 70, of which waited for: 40 -> 60; matrix products, arithmetic and copies ran while one was open for 1% -> 1% of each run, Pallas kernels for 0% -> 0%
where the time goes in v1:
time: 1030 us; the launch traced here: 1020 us
  local copies, waits for them, and re-layouts  328 us (32%)
  matrix products  227 us (22%)
  waiting for transfers between devices  197 us (19%)
  starting transfers between devices  170 us (17%)
  other arithmetic  72.7 us (7%)
  between operations  13.4 us (1%)
    another operation x45, local copies, waits for them, and re-layouts, correlate(): jnp.stack(pieces, axis=0).reshape(9 * channels, out_x, out_y, length_z)  223 us
    dot_general x30, matrix products, correlate(): jnp.einsum('ok,kxyz->oxyz', weight_block, patches, preferred_element_type...  130 us
    while x175, local copies, waits for them, and re-layouts  79.5 us
    ppermute x20, starting transfers between devices, extended(): lax.ppermute(tail, axis, [(i, (i + 1) % count) for i in range(ends)])  64.9 us
    all_to_all x5, waiting for transfers between devices, cascade(): lax.all_to_all(coil_img, 'space', split_axis=0, concat_axis=2, tiled=True)  57.6 us
    dot_general x40, matrix products, mult_rows(): jnp.einsum('kn,...nz->...kz', table, values, preferred_element_type=jnp.f...  49.7 us
    dot_general x40, matrix products, mult_last(): jnp.einsum('...n,nk->...k', values, table, preferred_element_type=jnp.flo...  47.4 us
    ppermute x15, waiting for transfers between devices, cascade(): lax.ppermute(sent, 'space', [(i_2, i_2 ^ step) for i_2 in range(size)])  39.6 us
  transfers between devices with their start and end apart: 70, of which 60 were waited for; matrix products, arithmetic and copies ran while one was open for 1% of the time, Pallas kernels for 0%

profile of v1, /device:TPU:20, one launch (start us, length us, event | category | flops | bytes accessed | tf_op | source)
XLA Modules:
  0.0 1023.4 jit_solution(10854624182477121311)
XLA Ops:
  10.2 1006.4 %while.20 = (s32[]{:T(128)}, f32[4,1,64,256]{3,0,2,1:T(4,128)S(1)}, f32[4,2,1,64,256]{4,3,1,0,2:T(8,128)}, pred[]{:T(512)}, s32[]{:T(128)}, /*index=5*/f32[4,2,1...) while((s32[]{:T(128)}, f32[4,1,64,256]{3,0,2,1:T(4,128)S(1)}, ...), condition=%wide.region_5.6_spmd.clone.clone, body=%wide.region_1.5_spmd.clone.clone.sunk | while | flops 1388957312 | bytes 366606848 | solution.py:224
  21.3 11.5 %all-to-all-done = bf16[8,2,64,256]{3,2,1,0:T(8,128)(2,1)S(1)} async-done(((bf16[8,2,64,256]{3,2,1,0:T(8,128)(2,1)}), bf16[8,2,64,256]{3,2,1,0:T(8,128)(2,1)S(1)}, u32[]{:S(2)}, u32[]{:S(2)}) %all-to-all-start) | async-done | bytes 524320 | tf_op jit(solution)/shard_map/while/body/eval_jaxpr/all_to_all | solution.py:161
  140.9 13.2 %copy.333 = bf16[9,32,1,64,256]{4,3,1,0,2:T(8,128)(2,1)} copy(bf16[9,32,1,64,256]{4,1,3,2,0:T(8,128)(2,1)} %fusion.431) | data formatting | bytes 18874368 | tf_op jit(solution)/shard_map/while/body/eval_jaxpr/stack | solution.py:103
  154.2 13.5 %copy.334 = bf16[9,32,1,64,256]{4,3,1,0,2:T(8,128)(2,1)} copy(bf16[9,32,1,64,256]{4,1,3,2,0:T(8,128)(2,1)} %copy-done.1) | data formatting | bytes 18874368 | tf_op jit(solution)/shard_map/while/body/eval_jaxpr/stack | solution.py:103
  181.9 13.3 %copy.335 = bf16[9,32,1,64,256]{4,3,1,0,2:T(8,128)(2,1)} copy(bf16[9,32,1,64,256]{4,1,3,2,0:T(8,128)(2,1)} %copy-done) | data formatting | bytes 18874368 | tf_op jit(solution)/shard_map/while/body/eval_jaxpr/stack | solution.py:103
  195.2 8.9 fusion.434
  223.3 11.5 %all-to-all-done = bf16[8,2,64,256]{3,2,1,0:T(8,128)(2,1)S(1)} async-done(((bf16[8,2,64,256]{3,2,1,0:T(8,128)(2,1)}), bf16[8,2,64,256]{3,2,1,0:T(8,128)(2,1)S(1)}, u32[]{:S(2)}, u32[]{:S(2)}) %all-to-all-start) | async-done | bytes 524320 | tf_op jit(solution)/shard_map/while/body/eval_jaxpr/all_to_all | solution.py:161
  341.8 13.2 %copy.333 = bf16[9,32,1,64,256]{4,3,1,0,2:T(8,128)(2,1)} copy(bf16[9,32,1,64,256]{4,1,3,2,0:T(8,128)(2,1)} %fusion.431) | data formatting | bytes 18874368 | tf_op jit(solution)/shard_map/while/body/eval_jaxpr/stack | solution.py:103
  355.1 13.5 %copy.334 = bf16[9,32,1,64,256]{4,3,1,0,2:T(8,128)(2,1)} copy(bf16[9,32,1,64,256]{4,1,3,2,0:T(8,128)(2,1)} %copy-done.1) | data formatting | bytes 18874368 | tf_op jit(solution)/shard_map/while/body/eval_jaxpr/stack | solution.py:103
  382.8 13.3 %copy.335 = bf16[9,32,1,64,256]{4,3,1,0,2:T(8,128)(2,1)} copy(bf16[9,32,1,64,256]{4,1,3,2,0:T(8,128)(2,1)} %copy-done) | data formatting | bytes 18874368 | tf_op jit(solution)/shard_map/while/body/eval_jaxpr/stack | solution.py:103
  396.1 8.9 fusion.434
  424.2 11.5 %all-to-all-done = bf16[8,2,64,256]{3,2,1,0:T(8,128)(2,1)S(1)} async-done(((bf16[8,2,64,256]{3,2,1,0:T(8,128)(2,1)}), bf16[8,2,64,256]{3,2,1,0:T(8,128)(2,1)S(1)}, u32[]{:S(2)}, u32[]{:S(2)}) %all-to-all-start) | async-done | bytes 524320 | tf_op jit(solution)/shard_map/while/body/eval_jaxpr/all_to_all | solution.py:161
  542.7 13.2 %copy.333 = bf16[9,32,1,64,256]{4,3,1,0,2:T(8,128)(2,1)} copy(bf16[9,32,1,64,256]{4,1,3,2,0:T(8,128)(2,1)} %fusion.431) | data formatting | bytes 18874368 | tf_op jit(solution)/shard_map/while/body/eval_jaxpr/stack | solution.py:103
  555.9 13.5 %copy.334 = bf16[9,32,1,64,256]{4,3,1,0,2:T(8,128)(2,1)} copy(bf16[9,32,1,64,256]{4,1,3,2,0:T(8,128)(2,1)} %copy-done.1) | data formatting | bytes 18874368 | tf_op jit(solution)/shard_map/while/body/eval_jaxpr/stack | solution.py:103
  583.7 13.3 %copy.335 = bf16[9,32,1,64,256]{4,3,1,0,2:T(8,128)(2,1)} copy(bf16[9,32,1,64,256]{4,1,3,2,0:T(8,128)(2,1)} %copy-done) | data formatting | bytes 18874368 | tf_op jit(solution)/shard_map/while/body/eval_jaxpr/stack | solution.py:103
  597.0 8.9 fusion.434
  625.1 11.5 %all-to-all-done = bf16[8,2,64,256]{3,2,1,0:T(8,128)(2,1)S(1)} async-done(((bf16[8,2,64,256]{3,2,1,0:T(8,128)(2,1)}), bf16[8,2,64,256]{3,2,1,0:T(8,128)(2,1)S(1)}, u32[]{:S(2)}, u32[]{:S(2)}) %all-to-all-start) | async-done | bytes 524320 | tf_op jit(solution)/shard_map/while/body/eval_jaxpr/all_to_all | solution.py:161
  743.6 13.2 %copy.333 = bf16[9,32,1,64,256]{4,3,1,0,2:T(8,128)(2,1)} copy(bf16[9,32,1,64,256]{4,1,3,2,0:T(8,128)(2,1)} %fusion.431) | data formatting | bytes 18874368 | tf_op jit(solution)/shard_map/while/body/eval_jaxpr/stack | solution.py:103
  756.8 13.5 %copy.334 = bf16[9,32,1,64,256]{4,3,1,0,2:T(8,128)(2,1)} copy(bf16[9,32,1,64,256]{4,1,3,2,0:T(8,128)(2,1)} %copy-done.1) | data formatting | bytes 18874368 | tf_op jit(solution)/shard_map/while/body/eval_jaxpr/stack | solution.py:103
  784.6 13.3 %copy.335 = bf16[9,32,1,64,256]{4,3,1,0,2:T(8,128)(2,1)} copy(bf16[9,32,1,64,256]{4,1,3,2,0:T(8,128)(2,1)} %copy-done) | data formatting | bytes 18874368 | tf_op jit(solution)/shard_map/while/body/eval_jaxpr/stack | solution.py:103
  826.0 11.5 %all-to-all-done = bf16[8,2,64,256]{3,2,1,0:T(8,128)(2,1)S(1)} async-done(((bf16[8,2,64,256]{3,2,1,0:T(8,128)(2,1)}), bf16[8,2,64,256]{3,2,1,0:T(8,128)(2,1)S(1)}, u32[]{:S(2)}, u32[]{:S(2)}) %all-to-all-start) | async-done | bytes 524320 | tf_op jit(solution)/shard_map/while/body/eval_jaxpr/all_to_all | solution.py:161
  944.4 13.2 %copy.333 = bf16[9,32,1,64,256]{4,3,1,0,2:T(8,128)(2,1)} copy(bf16[9,32,1,64,256]{4,1,3,2,0:T(8,128)(2,1)} %fusion.431) | data formatting | bytes 18874368 | tf_op jit(solution)/shard_map/while/body/eval_jaxpr/stack | solution.py:103
  957.7 13.5 %copy.334 = bf16[9,32,1,64,256]{4,3,1,0,2:T(8,128)(2,1)} copy(bf16[9,32,1,64,256]{4,1,3,2,0:T(8,128)(2,1)} %copy-done.1) | data formatting | bytes 18874368 | tf_op jit(solution)/shard_map/while/body/eval_jaxpr/stack | solution.py:103
  985.4 13.3 %copy.335 = bf16[9,32,1,64,256]{4,3,1,0,2:T(8,128)(2,1)} copy(bf16[9,32,1,64,256]{4,1,3,2,0:T(8,128)(2,1)} %copy-done) | data formatting | bytes 18874368 | tf_op jit(solution)/shard_map/while/body/eval_jaxpr/stack | solution.py:103
  (683 shorter events, 720.5 us)
Async XLA Ops:
  16.1 16.7 %all-to-all-start = ((bf16[8,2,64,256]{3,2,1,0:T(8,128)(2,1)}), bf16[8,2,64,256]{3,2,1,0:T(8,128)(2,1)S(1)}, u32[]{:S(2)}, u32[]{:S(2)}) async-start(bf16[8,2,64,256]{3,2,1,0:T(8,128)(2,1)} %pad_maximum_fusion.24), calls=%async_computation | async-start | bytes 1048576 | tf_op jit(solution)/shard_map/while/body/eval_jaxpr/all_to_all | solution.py:161
  21.3 55.5 %reduce-scatter.2.cloned.1.call-start = ((), (), s32[]{:S(2)}) async-start(), calls=%async_computation.2 | async-start | bytes 393216 | tf_op jit(solution)/shard_map/while/body/eval_jaxpr/reduce_scatter | solution.py:195
  52.7 10.5 %collective-permute-start = (bf16[2,2,64,256]{3,2,1,0:T(8,128)(2,1)S(1)}, bf16[2,2,64,256]{3,2,1,0:T(8,128)(2,1)S(1)}, u32[]{:S(2)}, u32[]{:S(2)}) collective-permute-start(bf16[2,2,64,256]{3,2,1,0:T(8,128)(2,1)S(1)} %bitcast.629), channel_id=1, source_target_pairs={{0,3},{1,2},{2,1},{3,0},{4,7},{5,6},{6,5},{7,4},{8,11},{9,10},{10,... | collective-permute-start | bytes 393224 | tf_op jit(solution)/shard_map/while/body/eval_jaxpr/ppermute | solution.py:179
  53.4 11.2 %collective-permute-start.1 = (bf16[2,2,64,256]{3,2,1,0:T(8,128)(2,1)S(1)}, bf16[2,2,64,256]{3,2,1,0:T(8,128)(2,1)S(1)}, u32[]{:S(2)}, u32[]{:S(2)}) collective-permute-start(bf16[2,2,64,256]{3,2,1,0:T(8,128)(2,1)S(1)} %bitcast.630), channel_id=1, source_target_pairs={{0,2},{1,3},{2,0},{3,1},{4,6},{5,7},{6,4},{7,5},{8,10},{9,11},{10,... | collective-permute-start | bytes 393224 | tf_op jit(solution)/shard_map/while/body/eval_jaxpr/ppermute | solution.py:179
  57.6 8.1 collective-permute-start.2
  218.2 16.6 %all-to-all-start = ((bf16[8,2,64,256]{3,2,1,0:T(8,128)(2,1)}), bf16[8,2,64,256]{3,2,1,0:T(8,128)(2,1)S(1)}, u32[]{:S(2)}, u32[]{:S(2)}) async-start(bf16[8,2,64,256]{3,2,1,0:T(8,128)(2,1)} %pad_maximum_fusion.24), calls=%async_computation | async-start | bytes 1048576 | tf_op jit(solution)/shard_map/while/body/eval_jaxpr/all_to_all | solution.py:161
  223.3 54.4 %reduce-scatter.2.cloned.1.call-start = ((), (), s32[]{:S(2)}) async-start(), calls=%async_computation.2 | async-start | bytes 393216 | tf_op jit(solution)/shard_map/while/body/eval_jaxpr/reduce_scatter | solution.py:195
  254.4 10.4 %collective-permute-start = (bf16[2,2,64,256]{3,2,1,0:T(8,128)(2,1)S(1)}, bf16[2,2,64,256]{3,2,1,0:T(8,128)(2,1)S(1)}, u32[]{:S(2)}, u32[]{:S(2)}) collective-permute-start(bf16[2,2,64,256]{3,2,1,0:T(8,128)(2,1)S(1)} %bitcast.629), channel_id=1, source_target_pairs={{0,3},{1,2},{2,1},{3,0},{4,7},{5,6},{6,5},{7,4},{8,11},{9,10},{10,... | collective-permute-start | bytes 393224 | tf_op jit(solution)/shard_map/while/body/eval_jaxpr/ppermute | solution.py:179
  255.1 11.2 %collective-permute-start.1 = (bf16[2,2,64,256]{3,2,1,0:T(8,128)(2,1)S(1)}, bf16[2,2,64,256]{3,2,1,0:T(8,128)(2,1)S(1)}, u32[]{:S(2)}, u32[]{:S(2)}) collective-permute-start(bf16[2,2,64,256]{3,2,1,0:T(8,128)(2,1)S(1)} %bitcast.630), channel_id=1, source_target_pairs={{0,2},{1,3},{2,0},{3,1},{4,6},{5,7},{6,4},{7,5},{8,10},{9,11},{10,... | collective-permute-start | bytes 393224 | tf_op jit(solution)/shard_map/while/body/eval_jaxpr/ppermute | solution.py:179
  259.3 8.0 collective-permute-start.2
  419.1 16.6 %all-to-all-start = ((bf16[8,2,64,256]{3,2,1,0:T(8,128)(2,1)}), bf16[8,2,64,256]{3,2,1,0:T(8,128)(2,1)S(1)}, u32[]{:S(2)}, u32[]{:S(2)}) async-start(bf16[8,2,64,256]{3,2,1,0:T(8,128)(2,1)} %pad_maximum_fusion.24), calls=%async_computation | async-start | bytes 1048576 | tf_op jit(solution)/shard_map/while/body/eval_jaxpr/all_to_all | solution.py:161
  424.2 54.4 %reduce-scatter.2.cloned.1.call-start = ((), (), s32[]{:S(2)}) async-start(), calls=%async_computation.2 | async-start | bytes 393216 | tf_op jit(solution)/shard_map/while/body/eval_jaxpr/reduce_scatter | solution.py:195
  455.3 10.5 %collective-permute-start = (bf16[2,2,64,256]{3,2,1,0:T(8,128)(2,1)S(1)}, bf16[2,2,64,256]{3,2,1,0:T(8,128)(2,1)S(1)}, u32[]{:S(2)}, u32[]{:S(2)}) collective-permute-start(bf16[2,2,64,256]{3,2,1,0:T(8,128)(2,1)S(1)} %bitcast.629), channel_id=1, source_target_pairs={{0,3},{1,2},{2,1},{3,0},{4,7},{5,6},{6,5},{7,4},{8,11},{9,10},{10,... | collective-permute-start | bytes 393224 | tf_op jit(solution)/shard_map/while/body/eval_jaxpr/ppermute | solution.py:179
  456.0 11.2 %collective-permute-start.1 = (bf16[2,2,64,256]{3,2,1,0:T(8,128)(2,1)S(1)}, bf16[2,2,64,256]{3,2,1,0:T(8,128)(2,1)S(1)}, u32[]{:S(2)}, u32[]{:S(2)}) collective-permute-start(bf16[2,2,64,256]{3,2,1,0:T(8,128)(2,1)S(1)} %bitcast.630), channel_id=1, source_target_pairs={{0,2},{1,3},{2,0},{3,1},{4,6},{5,7},{6,4},{7,5},{8,10},{9,11},{10,... | collective-permute-start | bytes 393224 | tf_op jit(solution)/shard_map/while/body/eval_jaxpr/ppermute | solution.py:179
  460.2 8.1 collective-permute-start.2
  619.9 16.7 %all-to-all-start = ((bf16[8,2,64,256]{3,2,1,0:T(8,128)(2,1)}), bf16[8,2,64,256]{3,2,1,0:T(8,128)(2,1)S(1)}, u32[]{:S(2)}, u32[]{:S(2)}) async-start(bf16[8,2,64,256]{3,2,1,0:T(8,128)(2,1)} %pad_maximum_fusion.24), calls=%async_computation | async-start | bytes 1048576 | tf_op jit(solution)/shard_map/while/body/eval_jaxpr/all_to_all | solution.py:161
  625.1 54.4 %reduce-scatter.2.cloned.1.call-start = ((), (), s32[]{:S(2)}) async-start(), calls=%async_computation.2 | async-start | bytes 393216 | tf_op jit(solution)/shard_map/while/body/eval_jaxpr/reduce_scatter | solution.py:195
  656.2 10.4 %collective-permute-start = (bf16[2,2,64,256]{3,2,1,0:T(8,128)(2,1)S(1)}, bf16[2,2,64,256]{3,2,1,0:T(8,128)(2,1)S(1)}, u32[]{:S(2)}, u32[]{:S(2)}) collective-permute-start(bf16[2,2,64,256]{3,2,1,0:T(8,128)(2,1)S(1)} %bitcast.629), channel_id=1, source_target_pairs={{0,3},{1,2},{2,1},{3,0},{4,7},{5,6},{6,5},{7,4},{8,11},{9,10},{10,... | collective-permute-start | bytes 393224 | tf_op jit(solution)/shard_map/while/body/eval_jaxpr/ppermute | solution.py:179
  656.9 11.2 %collective-permute-start.1 = (bf16[2,2,64,256]{3,2,1,0:T(8,128)(2,1)S(1)}, bf16[2,2,64,256]{3,2,1,0:T(8,128)(2,1)S(1)}, u32[]{:S(2)}, u32[]{:S(2)}) collective-permute-start(bf16[2,2,64,256]{3,2,1,0:T(8,128)(2,1)S(1)} %bitcast.630), channel_id=1, source_target_pairs={{0,2},{1,3},{2,0},{3,1},{4,6},{5,7},{6,4},{7,5},{8,10},{9,11},{10,... | collective-permute-start | bytes 393224 | tf_op jit(solution)/shard_map/while/body/eval_jaxpr/ppermute | solution.py:179
  820.8 16.6 %all-to-all-start = ((bf16[8,2,64,256]{3,2,1,0:T(8,128)(2,1)}), bf16[8,2,64,256]{3,2,1,0:T(8,128)(2,1)S(1)}, u32[]{:S(2)}, u32[]{:S(2)}) async-start(bf16[8,2,64,256]{3,2,1,0:T(8,128)(2,1)} %pad_maximum_fusion.24), calls=%async_computation | async-start | bytes 1048576 | tf_op jit(solution)/shard_map/while/body/eval_jaxpr/all_to_all | solution.py:161
  826.0 54.4 %reduce-scatter.2.cloned.1.call-start = ((), (), s32[]{:S(2)}) async-start(), calls=%async_computation.2 | async-start | bytes 393216 | tf_op jit(solution)/shard_map/while/body/eval_jaxpr/reduce_scatter | solution.py:195
  857.1 10.5 %collective-permute-start = (bf16[2,2,64,256]{3,2,1,0:T(8,128)(2,1)S(1)}, bf16[2,2,64,256]{3,2,1,0:T(8,128)(2,1)S(1)}, u32[]{:S(2)}, u32[]{:S(2)}) collective-permute-start(bf16[2,2,64,256]{3,2,1,0:T(8,128)(2,1)S(1)} %bitcast.629), channel_id=1, source_target_pairs={{0,3},{1,2},{2,1},{3,0},{4,7},{5,6},{6,5},{7,4},{8,11},{9,10},{10,... | collective-permute-start | bytes 393224 | tf_op jit(solution)/shard_map/while/body/eval_jaxpr/ppermute | solution.py:179
  857.8 11.2 %collective-permute-start.1 = (bf16[2,2,64,256]{3,2,1,0:T(8,128)(2,1)S(1)}, bf16[2,2,64,256]{3,2,1,0:T(8,128)(2,1)S(1)}, u32[]{:S(2)}, u32[]{:S(2)}) collective-permute-start(bf16[2,2,64,256]{3,2,1,0:T(8,128)(2,1)S(1)} %bitcast.630), channel_id=1, source_target_pairs={{0,2},{1,3},{2,0},{3,1},{4,6},{5,7},{6,4},{7,5},{8,10},{9,11},{10,... | collective-permute-start | bytes 393224 | tf_op jit(solution)/shard_map/while/body/eval_jaxpr/ppermute | solution.py:179
  862.0 8.1 collective-permute-start.2
  (94 other events, 826.2 us)
Sparse Core Ops, SparseCore 0:
  67.5 9.3 reduce-scatter.1
  269.2 8.4 reduce-scatter.1
  470.1 8.4 reduce-scatter.1
  671.0 8.4 reduce-scatter.1
  871.9 8.4 reduce-scatter.1
